TPU v7x, 256 devices: a whole 4x4x8 slice. The times are simulated.
256 devices in a mesh: dp: 32 (over x, y, core), mp: 8 (over z).
Axes of the slice: x: 4, y: 4, z: 8, core: 2. Of those that a mesh axis runs over, the one named last changes fastest.
Arguments:
- weight: bfloat16 [1024, 128, 128], P(('dp', 'mp')), may hold values from -6 to 6
- moment_one: float32 [1024, 128, 128], P(('dp', 'mp')), may hold values from -1.8 to 1.8
- moment_two: float32 [1024, 128, 128], P(('dp', 'mp')), may hold values from 0.01 to 1
- block_row: int32 [1024], P(('dp', 'mp')), may hold values from 0 to 63, as said below
- block_col: int32 [1024], P(('dp', 'mp')), may hold values from 0 to 27
- dest_slot: int32 [1024], P(('dp', 'mp')), may hold values from -1 to 127, as said below
- tokens: bfloat16 [4096, 8192], P('dp', 'mp'), may hold values from -6 to 6
- upstream: bfloat16 [4096, 28672], P('dp', 'mp'), may hold values from -6 to 6
Outputs:
- new_weight: bfloat16 [1024, 128, 128], P(('dp', 'mp'))
- new_first: float32 [1024, 128, 128], P(('dp', 'mp'))
- new_second: float32 [1024, 128, 128], P(('dp', 'mp'))
- hidden_out: bfloat16 [4096, 28672], P('dp', 'mp')
- input_grad: bfloat16 [4096, 8192], P('dp', 'mp')
Inputs may be any that keep to these rules, and one draw needn't show every extreme that they name: Within one tensor slice the pairs (block_row, block_col) are distinct. `dest_slot`: within one tensor slice the non-negative values are distinct; slots d * 4 to (d + 1) * 4 - 1 belong to dp index d, and a block held by dp index d goes to d - 1, d or d + 1; at most 2 blocks of one device go to each neighbour, and in every slice some pair of neighbours exchanges exactly 2 blocks each way.
All inputs are finite; a program needn't handle non-finite values.
Results may differ from a plain program's by a relative error of at most 0.0055.
Values may be sent and summed in bfloat16 or wider, within the bound.
A program may use at most 128 MiB of HBM per device.

v0:
```python
import math
import jax
import jax.numpy as jnp
from jax import lax
from jax.sharding import PartitionSpec as P

D = 8192
learn_rate = 0.02
beta_first = 0.9
beta_second = 0.95
epsilon = 1e-08
highest = lax.Precision.HIGHEST


def with_halo(shard, sides, width):
    for axis, dim in sides:
        size, length = (lax.axis_size(axis), shard.shape[dim])
        up = [(i, (i + 1) % size) for i in range(size - 1)]
        down = [(j, i) for i, j in up]
        last = lax.slice_in_dim(shard, length - width, length, axis=dim)
        initial = lax.slice_in_dim(shard, 0, width, axis=dim)
        before = lax.ppermute(last, axis, up)
        after = lax.ppermute(initial, axis, down)
        shard = jnp.concatenate([before, shard, after], axis=dim)
    return shard


def adam_update(gradient, weights, first_moment, second_moment):
    first_new = beta_first * first_moment + (1.0 - beta_first) * gradient
    second_new = beta_second * second_moment + (1.0 - beta_second) * gradient * gradient
    stepped = weights - learn_rate * first_new / (jnp.sqrt(second_new) + epsilon)
    return (stepped, first_new, second_new)


def moving_plan(dest_part, goal, kept_dev, half_slots):
    chosen = (dest_part >= 0) & (dest_part // kept_dev == goal)
    order_rank = jnp.cumsum(chosen.astype(jnp.int32)) - 1
    select = (
        (order_rank[None, :] == jnp.arange(half_slots, dtype=jnp.int32)[:, None]) & chosen[None, :]
    ).astype(jnp.float32)
    offsets = (
        jnp.dot(select, (dest_part % kept_dev + 1).astype(jnp.float32), precision=highest) - 1.0
    )
    return (select, offsets)


def relocate(stacked, all_dest):
    kept_dev = stacked.shape[0]
    half_slots = kept_dev // 2
    own_index = lax.axis_index("dp")
    last_index = lax.axis_size("dp") - 1
    own_dest = lax.dynamic_slice_in_dim(all_dest, own_index * kept_dev, kept_dev)
    left_dest = lax.dynamic_slice_in_dim(
        all_dest, jnp.maximum(own_index - 1, 0) * kept_dev, kept_dev
    )
    right_dest = lax.dynamic_slice_in_dim(
        all_dest, jnp.minimum(own_index + 1, last_index) * kept_dev, kept_dev
    )
    send_left, unused_left = moving_plan(own_dest, own_index - 1, kept_dev, half_slots)
    send_right, unused_right = moving_plan(own_dest, own_index + 1, kept_dev, half_slots)
    outgoing = jnp.dot(jnp.concatenate([send_left, send_right], axis=0), stacked, precision=highest)
    padded = with_halo(outgoing.astype(jnp.bfloat16), (("dp", 0),), half_slots).astype(
        outgoing.dtype
    )
    from_left = padded[:half_slots]
    from_right = padded[3 * half_slots :]
    unused_one, left_offsets = moving_plan(left_dest, own_index, kept_dev, half_slots)
    unused_two, right_offsets = moving_plan(right_dest, own_index, kept_dev, half_slots)
    left_offsets = jnp.where(own_index > 0, left_offsets, -1.0)
    right_offsets = jnp.where(own_index < last_index, right_offsets, -1.0)
    staying = (own_dest >= 0) & (own_dest // kept_dev == own_index)
    stay_offsets = jnp.where(staying, own_dest % kept_dev, -1).astype(jnp.float32)
    places = jnp.concatenate([stay_offsets, left_offsets, right_offsets])
    slot_hot = (jnp.arange(kept_dev, dtype=jnp.float32)[:, None] == places[None, :]).astype(
        jnp.float32
    )
    return jnp.dot(
        slot_hot, jnp.concatenate([stacked, from_left, from_right], axis=0), precision=highest
    )


def body(weight, moment_one, moment_two, block_row, block_col, dest_slot, tokens, upstream):
    kept_dev = weight.shape[0]
    block_side = weight.shape[1]
    flat_size = block_side * block_side
    grad_scale = 1.0 / math.sqrt(D)
    features = lax.all_gather(tokens, "mp", axis=1, tiled=True)
    all_weight, all_rows, all_cols, all_dest = (
        lax.all_gather(weight, "dp", axis=0, tiled=True),
        lax.all_gather(block_row, "dp", axis=0, tiled=True),
        lax.all_gather(block_col, "dp", axis=0, tiled=True),
        lax.all_gather(dest_slot, "dp", axis=0, tiled=True),
    )
    token_rows = features.shape[0]
    block_rows = features.shape[1] // block_side
    block_cols = upstream.shape[1] // block_side
    x_blocks = jnp.take(features.reshape(token_rows, block_rows, block_side), all_rows, axis=1)
    d_blocks = jnp.take(upstream.reshape(token_rows, block_cols, block_side), all_cols, axis=1)
    forward = jnp.einsum("tbk,bkj->btj", x_blocks, all_weight, preferred_element_type=jnp.float32)
    col_sums = jax.ops.segment_sum(forward, all_cols, num_segments=block_cols)
    hidden_out = (
        (jnp.swapaxes(col_sums, 0, 1) * grad_scale)
        .reshape(token_rows, block_cols * block_side)
        .astype(jnp.bfloat16)
    )
    backward = jnp.einsum("tbj,bkj->btk", d_blocks, all_weight, preferred_element_type=jnp.float32)
    row_sums = jax.ops.segment_sum(backward, all_rows, num_segments=block_rows)
    partial_in = (jnp.swapaxes(row_sums, 0, 1) * grad_scale).reshape(
        token_rows, block_rows * block_side
    )
    input_grad = lax.psum_scatter(partial_in, "mp", scatter_dimension=1, tiled=True).astype(
        jnp.bfloat16
    )
    old_weight = weight.reshape(kept_dev, flat_size).astype(jnp.float32)
    old_first = moment_one.reshape(kept_dev, flat_size)
    old_second = moment_two.reshape(kept_dev, flat_size)
    gradient = (
        lax.psum_scatter(
            (
                jnp.einsum("tbk,tbj->bkj", x_blocks, d_blocks, preferred_element_type=jnp.float32)
                * grad_scale
            ).astype(jnp.bfloat16),
            "dp",
            scatter_dimension=0,
            tiled=True,
        )
        .astype(jnp.float32)
        .reshape(kept_dev, flat_size)
    )
    held_weight, held_first, held_second = adam_update(gradient, old_weight, old_first, old_second)
    moved = relocate(jnp.concatenate([held_weight, held_first, held_second], axis=1), all_dest)
    stepped = moved[:, :flat_size]
    first_new = moved[:, flat_size : 2 * flat_size]
    second_new = moved[:, 2 * flat_size :]
    new_weight = stepped.astype(jnp.bfloat16).reshape(kept_dev, block_side, block_side)
    new_first = first_new.reshape(kept_dev, block_side, block_side)
    new_second = second_new.reshape(kept_dev, block_side, block_side)
    return (new_weight, new_first, new_second, hidden_out, input_grad)


def solution(mesh):
    return jax.shard_map(
        body,
        mesh=mesh,
        in_specs=(
            P(("dp", "mp"), None, None),
            P(("dp", "mp"), None, None),
            P(("dp", "mp"), None, None),
            P(("dp", "mp")),
            P(("dp", "mp")),
            P(("dp", "mp")),
            P("dp", "mp"),
            P("dp", "mp"),
        ),
        out_specs=(
            P(("dp", "mp"), None, None),
            P(("dp", "mp"), None, None),
            P(("dp", "mp"), None, None),
            P("dp", "mp"),
            P("dp", "mp"),
        ),
        check_vma=False,
    )
```

profile of v0, /device:TPU:1, one launch (start us, length us, event | category | flops | bytes accessed | tf_op | source)
XLA Modules:
  0.0 266.2 jit_solution(6325529828140879658)
XLA Ops:
  7.3 1.8 copy.28
  9.1 0.7 all-gather.5.cloned.1.call-update
  9.9 1.6 copy.30
  14.1 14.4 %all-reduce.3 = (s32[128]{0:T(128)S(1)}, s32[128]{0:T(128)S(1)}, s32[128]{0:T(128)S(1)}) all-reduce(s32[128]{0:T(128)S(1)} %dynamic-update-slice.1, s32[128]{0:T(128)S(1)} %dynamic-update-slice.2, s32[128]{0:T(128)S(1)} %dynamic-update-slice), channel_id=1, replica_groups=mesh['dp'=32,'mp'=8] {'dp'}, use_global_device_ids=true, to_apply=%add.1 | all-reduce | flops 384 | bytes 3072
  28.5 3.1 %gather_fusion.1 = bf16[128,128,128]{2,1,0:T(8,128)(2,1)} fusion(bf16[128,28,128]{2,0,1:T(8,128)(2,1)S(1)} %copy.31, s32[1024]{0:T(1024)S(1)} %pad_clamp_fusion), kind=kCustom, calls=%fused_computation.1 | custom fusion | bytes 8389120 | tf_op jit(solution)/shard_map/jit(_take)/gather | solution.py:98
  31.6 19.3 %all-gather.3.cloned.1.call-done = bf16[128,8192]{0,1:T(8,128)(2,1)} async-done(((bf16[128,1024]{0,1:T(8,128)(2,1)}), bf16[128,8192]{0,1:T(8,128)(2,1)}) %all-gather.3.cloned.1.call-update) | async-done | bytes 2097168 | tf_op jit(solution)/shard_map/all_gather | solution.py:87
  50.9 3.2 %copy.29 = bf16[128,64,128]{2,0,1:T(8,128)(2,1)S(1)} copy(bf16[128,64,128]{0,2,1:T(8,128)(2,1)} %bitcast.100) | data formatting | bytes 4194304 | tf_op jit(solution)/shard_map/reshape | solution.py:97
  54.1 3.0 %gather_fusion = bf16[128,128,128]{2,1,0:T(8,128)(2,1)} fusion(bf16[128,64,128]{2,0,1:T(8,128)(2,1)S(1)} %copy.29, s32[1024]{0:T(1024)S(1)} %pad_clamp_fusion.1), kind=kCustom, calls=%fused_computation | custom fusion | bytes 8389120 | tf_op jit(solution)/shard_map/jit(_take)/gather | solution.py:97
  57.1 7.5 %multiply_convert_fusion = bf16[128,128,128]{2,1,0:T(8,128)(2,1)} fusion(bf16[128,128,128]{2,1,0:T(8,128)(2,1)} %gather_fusion, pred[128]{0:T(512)(128)(4,1)S(1)} %get-tuple-element.48, bf16[128,128,128]{2,1,0:T(8,128)(2,1)} %gather_fusion.1, pred[128]{0:T(512)(128)(4,1)S(1)} %get-tuple-element.47), kind=kOutput, calls=%fused_computation.5 | convolution fusion | flops 545259520 | bytes 12583168 | tf_op jit(solution)/shard_map/tbk,tbj->bkj/dot_general | solution.py:120
  66.4 41.3 %all-gather.5.cloned.1.call-done = bf16[128,128,128]{2,1,0:T(8,128)(2,1)} async-done(((bf16[4,128,128]{2,1,0:T(8,128)(2,1)}), bf16[128,128,128]{2,1,0:T(8,128)(2,1)}) %all-gather.5.cloned.1.call-update) | async-done | bytes 4194320 | tf_op jit(solution)/shard_map/all_gather | solution.py:89
  107.7 9.8 %fusion = f32[128,128,128]{2,1,0:T(8,128)} fusion(bf16[128,128,128]{2,1,0:T(8,128)(2,1)} %all-gather.5.cloned.1.call-done, bf16[128,128,128]{2,1,0:T(8,128)(2,1)} %gather_fusion.1, pred[128]{0:T(512)(128)(4,1)S(1)} %get-tuple-element.47), kind=kOutput, calls=%fused_computation.6 | convolution fusion | flops 538968064 | bytes 16777344 | tf_op jit(solution)/shard_map/tbj,bkj->btk/dot_general | solution.py:106
  117.4 2.5 broadcast_in_dim.60
  119.9 27.1 %scatter_fusion.1 = f32[64,128,128]{2,1,0:T(8,128)} fusion(f32[64,128,128]{2,1,0:T(8,128)} %broadcast_in_dim.60, s32[128]{0:T(128)S(1)} %get-tuple-element.20, f32[128,128,128]{2,1,0:T(8,128)} %fusion), kind=kCustom, calls=%fused_computation.3 | custom fusion | flops 2097152 | bytes 25166336 | tf_op jit(solution)/shard_map/scatter-add | solution.py:107
  147.0 5.0 %multiply_bitcast_fusion = f32[128,64,128]{2,0,1:T(8,128)} fusion(f32[64,128,128]{2,1,0:T(8,128)} %scatter_fusion.1), kind=kLoop, calls=%fused_computation.13 | loop fusion | flops 1048576 | bytes 8388608 | tf_op jit(solution)/shard_map/mul | solution.py:108
  152.0 5.6 %copy.34 = f32[128,64,128]{0,2,1:T(8,128)} copy(f32[128,64,128]{2,0,1:T(8,128)} %multiply_bitcast_fusion) | data formatting | bytes 8388608 | tf_op jit(solution)/shard_map/mul | solution.py:108
  157.6 8.0 %fusion.4 = f32[128,128,128]{2,1,0:T(8,128)} fusion(bf16[128,128,128]{2,1,0:T(8,128)(2,1)} %all-gather.5.cloned.1.call-done, bf16[128,128,128]{2,1,0:T(8,128)(2,1)} %gather_fusion, pred[128]{0:T(512)(128)(4,1)S(1)} %get-tuple-element.48), kind=kOutput, calls=%fused_computation.10 | convolution fusion | flops 538968064 | bytes 16777344 | tf_op jit(solution)/shard_map/tbk,bkj->btj/dot_general | solution.py:99
  165.8 17.2 %scatter_fusion = f32[28,128,128]{2,1,0:T(8,128)S(1)} fusion(f32[28,128,128]{2,1,0:T(8,128)S(1)} %broadcast_in_dim.58, s32[128]{0:T(128)S(1)} %get-tuple-element.21, f32[128,128,128]{2,1,0:T(8,128)} %fusion.4), kind=kCustom, calls=%fused_computation.2 | custom fusion | flops 2097152 | bytes 25166336 | tf_op jit(solution)/shard_map/scatter-add | solution.py:100
  183.0 15.9 %reduce-scatter.3.cloned.1.call-done = bf16[4,128,128]{2,1,0:T(8,128)(2,1)} async-done(((bf16[128,128,128]{2,1,0:T(8,128)(2,1)}), bf16[4,128,128]{2,1,0:T(8,128)(2,1)}) %reduce-scatter.3.cloned.1.call-update) | async-done | bytes 131088 | tf_op jit(solution)/shard_map/reduce_scatter | solution.py:118
  198.9 0.9 convert_bitcast_fusion
  199.9 0.8 bitcast_subtract_fusion
  200.7 0.9 convolution_convert_fusion
  201.6 1.0 fusion.74
  202.7 4.3 %collective-permute-start.1 = (bf16[2,49152]{1,0:T(2,128)(2,1)}, bf16[2,49152]{1,0:T(2,128)(2,1)}, u32[]{:S(2)}, u32[]{:S(2)}) collective-permute-start(bf16[2,49152]{1,0:T(2,128)(2,1)} %get-tuple-element.42), channel_id=1, source_target_pairs={{8,0},{16,8},{24,16},{32,24},{40,32},{48,40},{56,48},{64,56},{72,6... | collective-permute-start | bytes 589832 | tf_op jit(solution)/shard_map/ppermute | solution.py:23
  206.9 2.9 %collective-permute-start = (bf16[2,49152]{1,0:T(2,128)(2,1)}, bf16[2,49152]{1,0:T(2,128)(2,1)}, u32[]{:S(2)}, u32[]{:S(2)}) collective-permute-start(bf16[2,49152]{1,0:T(2,128)(2,1)} %get-tuple-element.41), channel_id=1, source_target_pairs={{0,8},{8,16},{16,24},{24,32},{32,40},{40,48},{48,56},{56,64},{64,7... | collective-permute-start | bytes 589832 | tf_op jit(solution)/shard_map/ppermute | solution.py:22
  210.8 1.3 copy.35
  212.6 2.4 maximum_convert_fusion
  215.0 1.3 fusion.11
  217.0 0.7 copy.58
  217.7 0.7 copy.57
  218.4 39.3 %reduce-scatter.5.cloned.1.call-done = f32[128,1024]{0,1:T(8,128)} async-done(((f32[128,8192]{0,1:T(8,128)}), f32[128,1024]{0,1:T(8,128)}) %reduce-scatter.5.cloned.1.call-update) | async-done | bytes 524304 | tf_op jit(solution)/shard_map/reduce_scatter | solution.py:111
  257.8 1.1 convert_element_type.58
  258.9 0.9 copy.36
  (67 shorter events, 6.2 us)
Async XLA Ops:
  7.2 4.9 %copy-start.10 = (u32[256]{0:T(256)S(1)}, u32[256]{0:T(256)}, u32[]{:S(2)}) copy-start(u32[256]{0:T(256)} %constant.143) | copy-start | bytes 3076
  7.2 6.2 %copy-start.7 = (s32[4]{0:T(128)S(1)}, s32[4]{0:T(128)}, u32[]{:S(2)}) copy-start(s32[4]{0:T(128)} %param.11) | copy-start | bytes 52
  7.2 6.4 %copy-start.8 = (s32[4]{0:T(128)S(1)}, s32[4]{0:T(128)}, u32[]{:S(2)}) copy-start(s32[4]{0:T(128)} %param.12) | copy-start | bytes 52
  7.2 6.6 %copy-start.9 = (s32[4]{0:T(128)S(1)}, s32[4]{0:T(128)}, u32[]{:S(2)}) copy-start(s32[4]{0:T(128)} %param.13) | copy-start | bytes 52
  7.2 43.7 %all-gather.3.cloned.1.call-start = ((), (), s32[]{:S(2)}) async-start(), calls=%async_computation.2 | async-start | bytes 2359296 | tf_op jit(solution)/shard_map/all_gather | solution.py:87
  9.1 98.6 %all-gather.5.cloned.1.call-start = ((), (), s32[]{:S(2)}) async-start(), calls=%async_computation.4 | async-start | bytes 4325376 | tf_op jit(solution)/shard_map/all_gather | solution.py:89
  9.8 189.1 %reduce-scatter.3.cloned.1.call-start = ((), (), s32[]{:S(2)}) async-start(), calls=%async_computation.3 | async-start | bytes 4325376 | tf_op jit(solution)/shard_map/reduce_scatter | solution.py:118
  64.6 1.7 copy-start
  64.6 1.7 copy-start.5
  64.6 1.8 copy-start.6
  64.6 193.2 %reduce-scatter.5.cloned.1.call-start = ((), (), s32[]{:S(2)}) async-start(), calls=%async_computation.5 | async-start | bytes 4718592 | tf_op jit(solution)/shard_map/reduce_scatter | solution.py:111
  200.7 6.3 %copy-start.1 = (f32[4,16384]{1,0:T(4,128)}, f32[4,16384]{1,0:T(4,128)S(1)}, u32[]{:S(2)}) copy-start(f32[4,16384]{1,0:T(4,128)S(1)} %get-tuple-element.35) | copy-start | bytes 786436
  200.7 6.3 %copy-start.3 = (f32[4,16384]{1,0:T(4,128)}, f32[4,16384]{1,0:T(4,128)S(1)}, u32[]{:S(2)}) copy-start(f32[4,16384]{1,0:T(4,128)S(1)} %get-tuple-element.36) | copy-start | bytes 786436
  202.7 9.4 %collective-permute-start.1 = (bf16[2,49152]{1,0:T(2,128)(2,1)}, bf16[2,49152]{1,0:T(2,128)(2,1)}, u32[]{:S(2)}, u32[]{:S(2)}) collective-permute-start(bf16[2,49152]{1,0:T(2,128)(2,1)} %get-tuple-element.42), channel_id=1, source_target_pairs={{8,0},{16,8},{24,16},{32,24},{40,32},{48,40},{56,48},{64,56},{72,6... | collective-permute-start | bytes 589832 | tf_op jit(solution)/shard_map/ppermute | solution.py:23
  206.9 5.6 %collective-permute-start = (bf16[2,49152]{1,0:T(2,128)(2,1)}, bf16[2,49152]{1,0:T(2,128)(2,1)}, u32[]{:S(2)}, u32[]{:S(2)}) collective-permute-start(bf16[2,49152]{1,0:T(2,128)(2,1)} %get-tuple-element.41), channel_id=1, source_target_pairs={{0,8},{8,16},{16,24},{24,32},{32,40},{40,48},{48,56},{56,64},{64,7... | collective-permute-start | bytes 589832 | tf_op jit(solution)/shard_map/ppermute | solution.py:22
  210.1 4.8 %copy-start.2 = (f32[4,16384]{1,0:T(4,128)S(1)}, f32[4,16384]{1,0:T(4,128)}, u32[]{:S(2)}) copy-start(f32[4,16384]{1,0:T(4,128)} %copy-done.1) | copy-start | bytes 786436
  210.1 4.8 %copy-start.4 = (f32[4,16384]{1,0:T(4,128)S(1)}, f32[4,16384]{1,0:T(4,128)}, u32[]{:S(2)}) copy-start(f32[4,16384]{1,0:T(4,128)} %copy-done.3) | copy-start | bytes 786436
Sparse Core Ops, SparseCore 0:
  10.4 40.4 all-gather.2
  53.4 54.1 all-gather.4
  111.6 87.2 reduce-scatter.2
  201.3 56.3 reduce-scatter.4
where the time goes:
time: 267 us; the launch traced here: 266 us
  waiting for transfers between devices  117 us (44%)
  other arithmetic  55.8 us (21%)
  local copies, waits for them, and re-layouts  28.9 us (11%)
  matrix products  27.8 us (10%)
  between operations  14.8 us (6%)
  blocking collectives  14.4 us (5%)
  starting transfers between devices  7.52 us (3%)
    all_gather x1, waiting for transfers between devices, body(): lax.all_gather(weight, 'dp', axis=0, tiled=True)  41.3 us
    reduce_scatter x1, waiting for transfers between devices, body(): lax.psum_scatter(partial_in, 'mp', scatter_dimension=1, tiled=True)  39.3 us
    scatter-add x1, other arithmetic, body(): row_sums = jax.ops.segment_sum(backward, all_rows, num_segments=block_rows)  27.1 us
    all_gather x1, waiting for transfers between devices, body(): features = lax.all_gather(tokens, 'mp', axis=1, tiled=True)  19.3 us
    scatter-add x1, other arithmetic, body(): col_sums = jax.ops.segment_sum(forward, all_cols, num_segments=block_cols)  17.2 us
    reduce_scatter x1, waiting for transfers between devices, body(): lax.psum_scatter((jnp.einsum('tbk,tbj->bkj', x_blocks, d_blocks, preferre...  15.9 us
    unnamed x1, blocking collectives  14.4 us
    dot_general x1, matrix products, body(): jnp.einsum('tbj,bkj->btk', d_blocks, all_weight, preferred_element_type=j...  9.78 us
  transfers between devices with their start and end apart: 6, of which 5 were waited for; matrix products, arithmetic and copies ran while one was open for 41% of the time, Pallas kernels for 0%

commit v1 on v0

--- a/solution.py
+++ b/solution.py
@@ -86,7 +86,15 @@
     grad_scale = 1.0 / math.sqrt(D)
     features = lax.all_gather(tokens, "mp", axis=1, tiled=True)
     all_weight, all_rows, all_cols, all_dest = (
-        lax.all_gather(weight, "dp", axis=0, tiled=True),
+        jnp.concatenate(
+            lax.all_to_all(
+                jnp.stack([weight for _ in range(lax.axis_size("dp"))], 0),
+                "dp",
+                concat_axis=0,
+                split_axis=0,
+            ),
+            0,
+        ),
         lax.all_gather(block_row, "dp", axis=0, tiled=True),
         lax.all_gather(block_col, "dp", axis=0, tiled=True),
         lax.all_gather(dest_slot, "dp", axis=0, tiled=True),

time: 267 us -> 276 us (1.034)
  starting transfers between devices: 7.52 us -> 20.3 us
  waiting for transfers between devices: 117 us -> 110 us
  local copies, waits for them, and re-layouts: 28.9 us -> 32.6 us
    all_to_all x0 -> x1, waiting for transfers between devices: none -> 57.3 us  [body(): lax.all_to_all(jnp.stack([weight for _ in range(lax.axis_size('dp'))], 0)...]
    all_gather x1 -> x0, waiting for transfers between devices: 41.3 us -> none  [body(): lax.all_gather(weight, 'dp', axis=0, tiled=True)]
    reduce_scatter x1, waiting for transfers between devices: 15.9 us -> 0.02 us  [body(): lax.psum_scatter((jnp.einsum('tbk,tbj->bkj', x_blocks, d_blocks, preferre...]
    all_to_all x0 -> x1, starting transfers between devices: none -> 11.9 us  [body(): lax.all_to_all(jnp.stack([weight for _ in range(lax.axis_size('dp'))], 0)...]
    reduce_scatter x1, waiting for transfers between devices: 39.3 us -> 31.8 us  [body(): lax.psum_scatter(partial_in, 'mp', scatter_dimension=1, tiled=True)]
    another operation x0 -> x1, local copies, waits for them, and re-layouts: none -> 2.98 us  [body(): jnp.stack([weight for _ in range(lax.axis_size('dp'))], 0)]
  transfers between devices with their start and end apart: 6 -> 6, of which waited for: 5 -> 4; matrix products, arithmetic and copies ran while one was open for 41% -> 35% of each run, Pallas kernels for 0% -> 0%
where the time goes in v1:
time: 276 us; the launch traced here: 275 us
  waiting for transfers between devices  110 us (40%)
  other arithmetic  55 us (20%)
  local copies, waits for them, and re-layouts  32.6 us (12%)
  matrix products  28 us (10%)
  starting transfers between devices  20.3 us (7%)
  between operations  14.8 us (5%)
  blocking collectives  14.4 us (5%)
    all_to_all x1, waiting for transfers between devices, body(): lax.all_to_all(jnp.stack([weight for _ in range(lax.axis_size('dp'))], 0)...  57.3 us
    reduce_scatter x1, waiting for transfers between devices, body(): lax.psum_scatter(partial_in, 'mp', scatter_dimension=1, tiled=True)  31.8 us
    scatter-add x1, other arithmetic, body(): row_sums = jax.ops.segment_sum(backward, all_rows, num_segments=block_rows)  26.5 us
    all_gather x1, waiting for transfers between devices, body(): features = lax.all_gather(tokens, 'mp', axis=1, tiled=True)  20.1 us
    scatter-add x1, other arithmetic, body(): col_sums = jax.ops.segment_sum(forward, all_cols, num_segments=block_cols)  17.1 us
    unnamed x1, blocking collectives  14.4 us
    all_to_all x1, starting transfers between devices, body(): lax.all_to_all(jnp.stack([weight for _ in range(lax.axis_size('dp'))], 0)...  11.9 us
    dot_general x1, matrix products, body(): jnp.einsum('tbj,bkj->btk', d_blocks, all_weight, preferred_element_type=j...  9.91 us
  transfers between devices with their start and end apart: 6, of which 4 were waited for; matrix products, arithmetic and copies ran while one was open for 35% of the time, Pallas kernels for 0%

profile of v1, /device:TPU:1, one launch (start us, length us, event | category | flops | bytes accessed | tf_op | source)
XLA Modules:
  0.0 274.8 jit_solution(7096065754359575980)
XLA Ops:
  7.3 1.8 copy.19
  9.1 1.6 copy.21
  13.3 14.4 %all-reduce.3 = (s32[128]{0:T(128)S(1)}, s32[128]{0:T(128)S(1)}, s32[128]{0:T(128)S(1)}) all-reduce(s32[128]{0:T(128)S(1)} %dynamic-update-slice.1, s32[128]{0:T(128)S(1)} %dynamic-update-slice.2, s32[128]{0:T(128)S(1)} %dynamic-update-slice), channel_id=1, replica_groups=mesh['dp'=32,'mp'=8] {'dp'}, use_global_device_ids=true, to_apply=%add.1 | all-reduce | flops 384 | bytes 3072
  27.8 3.0 %gather_fusion.1 = bf16[128,128,128]{2,1,0:T(8,128)(2,1)} fusion(bf16[128,28,128]{2,0,1:T(8,128)(2,1)S(1)} %copy.22, s32[1024]{0:T(1024)S(1)} %pad_clamp_fusion), kind=kCustom, calls=%fused_computation.1 | custom fusion | bytes 8389120 | tf_op jit(solution)/shard_map/jit(_take)/gather | solution.py:106
  30.8 20.1 %all-gather.2.cloned.1.call-done = bf16[128,8192]{0,1:T(8,128)(2,1)} async-done(((bf16[128,1024]{0,1:T(8,128)(2,1)}), bf16[128,8192]{0,1:T(8,128)(2,1)}) %all-gather.2.cloned.1.call-update) | async-done | bytes 2097168 | tf_op jit(solution)/shard_map/all_gather | solution.py:87
  50.9 3.2 %copy.20 = bf16[128,64,128]{2,0,1:T(8,128)(2,1)S(1)} copy(bf16[128,64,128]{0,2,1:T(8,128)(2,1)} %bitcast.101) | data formatting | bytes 4194304 | tf_op jit(solution)/shard_map/reshape | solution.py:105
  54.1 3.0 %gather_fusion = bf16[128,128,128]{2,1,0:T(8,128)(2,1)} fusion(bf16[128,64,128]{2,0,1:T(8,128)(2,1)S(1)} %copy.20, s32[1024]{0:T(1024)S(1)} %pad_clamp_fusion.1), kind=kCustom, calls=%fused_computation | custom fusion | bytes 8389120 | tf_op jit(solution)/shard_map/jit(_take)/gather | solution.py:105
  57.1 7.5 %multiply_convert_fusion = bf16[128,128,128]{2,1,0:T(8,128)(2,1)} fusion(bf16[128,128,128]{2,1,0:T(8,128)(2,1)} %gather_fusion, pred[128]{0:T(512)(128)(4,1)S(1)} %get-tuple-element.43, bf16[128,128,128]{2,1,0:T(8,128)(2,1)} %gather_fusion.1, pred[128]{0:T(512)(128)(4,1)S(1)} %get-tuple-element.42), kind=kOutput, calls=%fused_computation.5 | convolution fusion | flops 545259520 | bytes 12583168 | tf_op jit(solution)/shard_map/tbk,tbj->bkj/dot_general | solution.py:128
  64.6 0.9 copy-done
  65.5 3.0 %stack.2 = bf16[32,4,128,128]{3,2,1,0:T(8,128)(2,1)} broadcast(bf16[4,128,128]{2,1,0:T(8,128)(2,1)S(1)} %copy-done), dimensions={1,2,3} | broadcast | bytes 4325376 | tf_op jit(solution)/shard_map/stack | solution.py:91
  68.5 11.9 %all-to-all-start = ((bf16[32,4,128,128]{3,2,1,0:T(8,128)(2,1)}), bf16[32,4,128,128]{3,2,1,0:T(8,128)(2,1)}, u32[]{:S(2)}, u32[]{:S(2)}) async-start(bf16[32,4,128,128]{3,2,1,0:T(8,128)(2,1)} %stack.2), calls=%async_computation.1 | async-start | bytes 8388608 | tf_op jit(solution)/shard_map/all_to_all | solution.py:90
  82.2 57.3 %all-to-all-done = bf16[32,4,128,128]{3,2,1,0:T(8,128)(2,1)} async-done(((bf16[32,4,128,128]{3,2,1,0:T(8,128)(2,1)}), bf16[32,4,128,128]{3,2,1,0:T(8,128)(2,1)}, u32[]{:S(2)}, u32[]{:S(2)}) %all-to-all-start) | async-done | bytes 4194336 | tf_op jit(solution)/shard_map/all_to_all | solution.py:90
  139.5 9.9 %fusion = f32[128,128,128]{2,1,0:T(8,128)} fusion(bf16[128,128,128]{2,1,0:T(8,128)(2,1)} %bitcast.17, bf16[128,128,128]{2,1,0:T(8,128)(2,1)} %gather_fusion.1, pred[128]{0:T(512)(128)(4,1)S(1)} %get-tuple-element.42), kind=kOutput, calls=%fused_computation.6 | convolution fusion | flops 538968064 | bytes 16777344 | tf_op jit(solution)/shard_map/tbj,bkj->btk/dot_general | solution.py:114
  149.4 2.4 broadcast_in_dim.60
  151.8 26.5 %scatter_fusion.1 = f32[64,128,128]{2,1,0:T(8,128)} fusion(f32[64,128,128]{2,1,0:T(8,128)} %broadcast_in_dim.60, s32[128]{0:T(128)S(1)} %get-tuple-element.15, f32[128,128,128]{2,1,0:T(8,128)} %fusion), kind=kCustom, calls=%fused_computation.3 | custom fusion | flops 2097152 | bytes 25166336 | tf_op jit(solution)/shard_map/scatter-add | solution.py:115
  178.4 4.9 %multiply_bitcast_fusion = f32[128,64,128]{2,0,1:T(8,128)} fusion(f32[64,128,128]{2,1,0:T(8,128)} %scatter_fusion.1), kind=kLoop, calls=%fused_computation.13 | loop fusion | flops 1048576 | bytes 8388608 | tf_op jit(solution)/shard_map/mul | solution.py:116
  183.2 5.6 %copy.25 = f32[128,64,128]{0,2,1:T(8,128)} copy(f32[128,64,128]{2,0,1:T(8,128)} %multiply_bitcast_fusion) | data formatting | bytes 8388608 | tf_op jit(solution)/shard_map/mul | solution.py:116
  188.8 8.0 %fusion.4 = f32[128,128,128]{2,1,0:T(8,128)} fusion(bf16[128,128,128]{2,1,0:T(8,128)(2,1)} %bitcast.17, bf16[128,128,128]{2,1,0:T(8,128)(2,1)} %gather_fusion, pred[128]{0:T(512)(128)(4,1)S(1)} %get-tuple-element.43), kind=kOutput, calls=%fused_computation.10 | convolution fusion | flops 538968064 | bytes 16777344 | tf_op jit(solution)/shard_map/tbk,bkj->btj/dot_general | solution.py:107
  197.0 17.1 %scatter_fusion = f32[28,128,128]{2,1,0:T(8,128)S(1)} fusion(f32[28,128,128]{2,1,0:T(8,128)S(1)} %broadcast_in_dim.58, s32[128]{0:T(128)S(1)} %get-tuple-element.16, f32[128,128,128]{2,1,0:T(8,128)} %fusion.4), kind=kCustom, calls=%fused_computation.2 | custom fusion | flops 2097152 | bytes 25166336 | tf_op jit(solution)/shard_map/scatter-add | solution.py:108
  214.2 0.9 convert_bitcast_fusion
  215.1 0.8 bitcast_subtract_fusion
  215.9 0.9 convolution_convert_fusion
  216.8 1.0 fusion.74
  217.9 3.9 %collective-permute-start.1 = (bf16[2,49152]{1,0:T(2,128)(2,1)}, bf16[2,49152]{1,0:T(2,128)(2,1)}, u32[]{:S(2)}, u32[]{:S(2)}) collective-permute-start(bf16[2,49152]{1,0:T(2,128)(2,1)} %get-tuple-element.37), channel_id=1, source_target_pairs={{8,0},{16,8},{24,16},{32,24},{40,32},{48,40},{56,48},{64,56},{72,6... | collective-permute-start | bytes 589832 | tf_op jit(solution)/shard_map/ppermute | solution.py:23
  221.8 4.2 %collective-permute-start = (bf16[2,49152]{1,0:T(2,128)(2,1)}, bf16[2,49152]{1,0:T(2,128)(2,1)}, u32[]{:S(2)}, u32[]{:S(2)}) collective-permute-start(bf16[2,49152]{1,0:T(2,128)(2,1)} %get-tuple-element.36), channel_id=1, source_target_pairs={{0,8},{8,16},{16,24},{24,32},{32,40},{40,48},{48,56},{56,64},{64,7... | collective-permute-start | bytes 589832 | tf_op jit(solution)/shard_map/ppermute | solution.py:22
  227.0 1.3 copy.26
  228.7 2.4 maximum_convert_fusion
  231.1 1.3 fusion.11
  233.1 0.7 copy.49
  234.6 31.8 %reduce-scatter.5.cloned.1.call-done = f32[128,1024]{0,1:T(8,128)} async-done(((f32[128,8192]{0,1:T(8,128)}), f32[128,1024]{0,1:T(8,128)}) %reduce-scatter.5.cloned.1.call-update) | async-done | bytes 524304 | tf_op jit(solution)/shard_map/reduce_scatter | solution.py:119
  266.4 1.1 convert_element_type.58
  267.4 0.9 copy.27
  (67 shorter events, 6.9 us)
Async XLA Ops:
  7.2 4.2 %copy-start.10 = (u32[256]{0:T(256)S(1)}, u32[256]{0:T(256)}, u32[]{:S(2)}) copy-start(u32[256]{0:T(256)} %constant.143) | copy-start | bytes 3076
  7.2 5.4 %copy-start.7 = (s32[4]{0:T(128)S(1)}, s32[4]{0:T(128)}, u32[]{:S(2)}) copy-start(s32[4]{0:T(128)} %param.11) | copy-start | bytes 52
  7.2 5.7 %copy-start.8 = (s32[4]{0:T(128)S(1)}, s32[4]{0:T(128)}, u32[]{:S(2)}) copy-start(s32[4]{0:T(128)} %param.12) | copy-start | bytes 52
  7.2 5.9 %copy-start.9 = (s32[4]{0:T(128)S(1)}, s32[4]{0:T(128)}, u32[]{:S(2)}) copy-start(s32[4]{0:T(128)} %param.13) | copy-start | bytes 52
  7.2 43.7 %all-gather.2.cloned.1.call-start = ((), (), s32[]{:S(2)}) async-start(), calls=%async_computation.3 | async-start | bytes 2359296 | tf_op jit(solution)/shard_map/all_gather | solution.py:87
  9.1 205.1 %reduce-scatter.3.cloned.1.call-start = ((), (), s32[]{:S(2)}) async-start(), calls=%async_computation.4 | async-start | bytes 4325376 | tf_op jit(solution)/shard_map/reduce_scatter | solution.py:126
  64.6 0.9 copy-start
  68.5 13.6 %copy-start.5 = (f32[4,128,128]{2,1,0:T(8,128)S(1)}, f32[4,128,128]{2,1,0:T(8,128)}, u32[]{:S(2)}) copy-start(f32[4,128,128]{2,1,0:T(8,128)} %param.10) | copy-start | bytes 786436
  68.5 13.6 %copy-start.6 = (f32[4,128,128]{2,1,0:T(8,128)S(1)}, f32[4,128,128]{2,1,0:T(8,128)}, u32[]{:S(2)}) copy-start(f32[4,128,128]{2,1,0:T(8,128)} %param.9) | copy-start | bytes 786436
  68.5 71.0 %all-to-all-start = ((bf16[32,4,128,128]{3,2,1,0:T(8,128)(2,1)}), bf16[32,4,128,128]{3,2,1,0:T(8,128)(2,1)}, u32[]{:S(2)}, u32[]{:S(2)}) async-start(bf16[32,4,128,128]{3,2,1,0:T(8,128)(2,1)} %stack.2), calls=%async_computation.1 | async-start | bytes 8388608 | tf_op jit(solution)/shard_map/all_to_all | solution.py:90
  80.4 185.9 %reduce-scatter.5.cloned.1.call-start = ((), (), s32[]{:S(2)}) async-start(), calls=%async_computation.5 | async-start | bytes 4718592 | tf_op jit(solution)/shard_map/reduce_scatter | solution.py:119
  215.9 5.9 %copy-start.1 = (f32[4,16384]{1,0:T(4,128)}, f32[4,16384]{1,0:T(4,128)S(1)}, u32[]{:S(2)}) copy-start(f32[4,16384]{1,0:T(4,128)S(1)} %get-tuple-element.30) | copy-start | bytes 786436
  215.9 5.9 %copy-start.3 = (f32[4,16384]{1,0:T(4,128)}, f32[4,16384]{1,0:T(4,128)S(1)}, u32[]{:S(2)}) copy-start(f32[4,16384]{1,0:T(4,128)S(1)} %get-tuple-element.31) | copy-start | bytes 786436
  217.9 10.4 %collective-permute-start.1 = (bf16[2,49152]{1,0:T(2,128)(2,1)}, bf16[2,49152]{1,0:T(2,128)(2,1)}, u32[]{:S(2)}, u32[]{:S(2)}) collective-permute-start(bf16[2,49152]{1,0:T(2,128)(2,1)} %get-tuple-element.37), channel_id=1, source_target_pairs={{8,0},{16,8},{24,16},{32,24},{40,32},{48,40},{56,48},{64,56},{72,6... | collective-permute-start | bytes 589832 | tf_op jit(solution)/shard_map/ppermute | solution.py:23
  221.8 6.9 %collective-permute-start = (bf16[2,49152]{1,0:T(2,128)(2,1)}, bf16[2,49152]{1,0:T(2,128)(2,1)}, u32[]{:S(2)}, u32[]{:S(2)}) collective-permute-start(bf16[2,49152]{1,0:T(2,128)(2,1)} %get-tuple-element.36), channel_id=1, source_target_pairs={{0,8},{8,16},{16,24},{24,32},{32,40},{40,48},{48,56},{56,64},{64,7... | collective-permute-start | bytes 589832 | tf_op jit(solution)/shard_map/ppermute | solution.py:22
  226.3 4.8 %copy-start.2 = (f32[4,16384]{1,0:T(4,128)S(1)}, f32[4,16384]{1,0:T(4,128)}, u32[]{:S(2)}) copy-start(f32[4,16384]{1,0:T(4,128)} %copy-done.1) | copy-start | bytes 786436
  226.3 4.8 %copy-start.4 = (f32[4,16384]{1,0:T(4,128)S(1)}, f32[4,16384]{1,0:T(4,128)}, u32[]{:S(2)}) copy-start(f32[4,16384]{1,0:T(4,128)} %copy-done.3) | copy-start | bytes 786436
Sparse Core Ops, SparseCore 0:
  10.4 40.4 all-gather.1
  64.8 96.2 reduce-scatter.2
  214.2 52.0 reduce-scatter.4
